TPU v7x, 512 devices: a whole 4x8x8 slice. The times are simulated.
512 devices in a mesh: ctx: 16 (over z, core), tis: 8 (over y), rep: 4 (over x).
Axes of the slice: x: 4, y: 8, z: 8, core: 2. Of those that a mesh axis runs over, the one named last changes fastest.
Arguments:
- donor_feat: bfloat16 [4, 256, 256], P('rep', 'ctx'), may hold values from -6 to 6
- acceptor_feat: bfloat16 [4, 256, 256], P('rep', 'ctx'), may hold values from -6 to 6
- donor_pos: int32 [4, 256], P('rep', 'ctx'), may hold values from 0 to 65535
- acceptor_pos: int32 [4, 256], P('rep'), may hold values from 0 to 65535
- pair_mask: int32 [4, 256, 80], P('rep', 'ctx'), may hold values from 0 to 1
- targets: int32 [4, 256, 32], P('rep', 'ctx', 'tis'), may hold values from 0 to 80, as said below
- dist_table: bfloat16 [128, 256], replicated, may hold values from -3 to 3
- hidden_weights: bfloat16 [32, 256, 512], P('tis'), may hold values from -0.375 to 0.375
- output_weights: bfloat16 [32, 512], P('tis')
Outputs:
- donor_loss: float32 [4, 256, 32], P('rep', 'ctx', 'tis')
- grad_hidden: float32 [32, 256, 512], P('tis', ('ctx', 'rep'))
- grad_acceptor: float32 [4, 256, 256], P('rep', 'ctx')
Inputs may be any that keep to these rules, and one draw needn't show every extreme that they name: `targets`: each target is a valid slot of its donor, or 80 for no splice.
All inputs are finite; a program needn't handle non-finite values.
Results may differ from a plain program's by a relative error of at most 0.002.
The roundings to bfloat16 on the way count: a program that leaves them out, or rounds other values in their place, can miss the bound.
Values may be sent and summed in bfloat16 or wider, within the bound.
A program may use at most 64 MiB of HBM per device.

v0:
```python
import jax
import jax.numpy as jnp
from jax import lax
from jax.sharding import PartitionSpec as P

BLOCK_BP = 65536
SPAN_BLOCKS = 4
BIN_BP = 2048
BINS = 128


def passed_along(value, axis, steps):
    count = lax.axis_size(axis)
    first, last = (max(0, -steps), min(count, count - steps))
    return lax.ppermute(value, axis, [(source, source + steps) for source in range(first, last)])


def silu_grad(values):
    sig = jax.nn.sigmoid(values)
    return sig * (1.0 + values * (1.0 - sig))


def on_device(
    donor_feat,
    acceptor_feat,
    donor_pos,
    acceptor_pos,
    pair_mask,
    targets,
    dist_table,
    hidden_weights,
    output_weights,
):
    seq_dev, don_blk, width = donor_feat.shape
    acc_blk = acceptor_feat.shape[1]
    blocks = lax.axis_size("ctx")
    reach = SPAN_BLOCKS + 1
    slots = reach * acc_blk
    here = lax.axis_index("ctx")
    pieces = [acceptor_feat]
    current = acceptor_feat
    for offset in range(1, reach):
        current = passed_along(current, "ctx", -1)
        pieces.append(current)
    window = jnp.stack(pieces, axis=1).reshape(seq_dev, slots, width)
    pos_pad = jnp.concatenate(
        [acceptor_pos, jnp.zeros((seq_dev, SPAN_BLOCKS * acc_blk), jnp.int32)], axis=1
    )
    pos_win = lax.dynamic_slice_in_dim(pos_pad, here * acc_blk, slots, 1)
    slot_block = jnp.arange(slots, dtype=jnp.int32) // acc_blk
    inchain = here + slot_block < blocks
    dist = slot_block * BLOCK_BP + pos_win[:, None, :] - donor_pos[:, :, None]
    valid = (pair_mask > 0) & (dist > 0) & (dist <= SPAN_BLOCKS * BLOCK_BP) & inchain[None, None, :]
    bins = jnp.clip((dist - 1) // BIN_BP, 0, BINS - 1)
    lookup = (
        (bins[..., None] == jnp.arange(BINS, dtype=jnp.int32))
        .astype(jnp.bfloat16)
        .reshape(-1, BINS)
    )
    table = jnp.dot(lookup, dist_table, preferred_element_type=jnp.float32).reshape(
        seq_dev, don_blk, slots, width
    )
    pre = (
        donor_feat.astype(jnp.float32)[:, :, None, :] + window.astype(jnp.float32)[:, None] + table
    )
    flat = jax.nn.silu(pre).astype(jnp.bfloat16).reshape(-1, width)
    grad_pair = jnp.zeros((flat.shape[0], width), jnp.float32)
    losses = []
    fulls = []
    slot_ids = jnp.arange(slots, dtype=jnp.int32)
    for tissue in range(hidden_weights.shape[0]):
        w_in = hidden_weights[tissue]
        w_out = output_weights[tissue]
        goal = targets[:, :, tissue]
        hid = jnp.dot(flat, w_in, preferred_element_type=jnp.float32)
        act = jax.nn.silu(hid).astype(jnp.bfloat16)
        logits = jnp.dot(act, w_out, preferred_element_type=jnp.float32).reshape(
            seq_dev, don_blk, slots
        )
        masked = jnp.where(valid, logits, -jnp.inf)
        top = jnp.maximum(jnp.max(masked, axis=-1), 0.0)
        expo = jnp.exp(masked - top[..., None])
        total = jnp.sum(expo, axis=-1) + jnp.exp(-top)
        picked = jnp.take_along_axis(logits, jnp.minimum(goal, slots - 1)[..., None], axis=-1)[
            ..., 0
        ]
        picked = jnp.where(goal == slots, 0.0, picked)
        losses.append(top + jnp.log(total) - picked)
        onehot = (goal[..., None] == slot_ids).astype(jnp.float32)
        grad_logits = expo / total[..., None] - onehot
        grad_act = grad_logits.reshape(-1)[:, None] * w_out.astype(jnp.float32)[None, :]
        grad_hid = (grad_act * silu_grad(hid)).astype(jnp.bfloat16)
        grad_pair = grad_pair + lax.dot_general(
            grad_hid, w_in, (((1,), (1,)), ((), ())), preferred_element_type=jnp.float32
        )
        fulls.append(
            lax.dot_general(
                flat, grad_hid, (((0,), (0,)), ((), ())), preferred_element_type=jnp.float32
            )
        )
    stacked = jnp.stack(fulls, axis=1)
    grad_hidden = jnp.transpose(
        lax.psum_scatter(stacked, ("ctx", "rep"), scatter_dimension=0, tiled=True), (1, 0, 2)
    )
    grad_pre = grad_pair.reshape(seq_dev, don_blk, slots, width) * silu_grad(pre)
    contrib = jnp.sum(grad_pre, axis=1).reshape(seq_dev, reach, acc_blk, width)
    carried = contrib[:, reach - 1]
    for offset in range(reach - 2, -1, -1):
        carried = passed_along(carried, "ctx", 1) + contrib[:, offset]
    grad_acceptor = lax.psum(carried, "tis")
    donor_loss = jnp.stack(losses, axis=-1)
    return (donor_loss, grad_hidden, grad_acceptor)


def solution(mesh):
    placed = (
        P("rep", "ctx", None),
        P("rep", "ctx", None),
        P("rep", "ctx"),
        P("rep", None),
        P("rep", "ctx", None),
        P("rep", "ctx", "tis"),
        P(),
        P("tis", None, None),
        P("tis", None),
    )
    return jax.shard_map(
        on_device,
        mesh=mesh,
        in_specs=placed,
        out_specs=(P("rep", "ctx", "tis"), P("tis", ("ctx", "rep"), None), P("rep", "ctx", None)),
        check_vma=False,
    )
```

profile of v0, /device:TPU:8, one launch (start us, length us, event | category | flops | bytes accessed | tf_op | source)
XLA Modules:
  0.0 280.9 jit_solution(4810384354852864490)
XLA Ops:
  7.2 1.3 collective-permute-start
  8.5 0.7 constant_dynamic-update-slice_fusion.4
  9.2 0.7 bitcast_convert_fusion.1
  9.9 0.8 slice_bitcast_fusion.8
  10.8 0.9 slice_reduce_fusion.3
  11.6 0.8 bitcast_add_fusion.4
  12.4 0.7 fusion.28
  13.2 1.3 collective-permute-start.1
  14.6 2.4 collective-permute-done.1
  16.9 1.3 collective-permute-start.2
  18.2 3.9 %collective-permute-done.2 = bf16[1,16,256]{2,1,0:T(8,128)(2,1)S(1)} collective-permute-done((bf16[1,16,256]{2,1,0:T(8,128)(2,1)S(1)}, bf16[1,16,256]{2,1,0:T(8,128)(2,1)S(1)}, u32[]{:S(2)}, u32[]{:S(2)}) %collective-permute-start.2) | collective-permute-done | bytes 8224 | tf_op jit(solution)/shard_map/ppermute | solution.py:15
  22.2 1.3 collective-permute-start.3
  23.5 3.7 %collective-permute-done.3 = bf16[1,16,256]{2,1,0:T(8,128)(2,1)S(1)} collective-permute-done((bf16[1,16,256]{2,1,0:T(8,128)(2,1)S(1)}, bf16[1,16,256]{2,1,0:T(8,128)(2,1)S(1)}, u32[]{:S(2)}, u32[]{:S(2)}) %collective-permute-start.3) | collective-permute-done | bytes 8224 | tf_op jit(solution)/shard_map/ppermute | solution.py:15
  27.2 1.7 multiply_convert_fusion.8
  28.9 0.9 multiply_convert_fusion.7
  29.7 2.3 multiply_convert_fusion.4
  32.0 2.3 multiply_convert_fusion.5
  34.3 2.3 multiply_convert_fusion.6
  37.2 0.6 fusion.42
  37.7 0.6 fusion.44
  38.3 0.6 fusion.46
  39.5 1.0 multiply_convert_fusion.3
  40.5 1.4 convolution_bitcast_fusion.3
  41.9 2.5 fusion.10
  44.5 2.7 multiply_convert_fusion
  47.2 1.3 convolution_bitcast_fusion
  48.6 2.7 multiply_convert_fusion.1
  51.3 1.3 convolution_bitcast_fusion.1
  52.8 2.7 multiply_convert_fusion.2
  56.0 0.8 copy-done.1
  57.1 0.6 convolution_add_fusion.2
  57.7 0.6 convolution_add_fusion.1
  58.9 0.7 copy-done.5
  60.1 4.3 %collective-permute-start.4 = (f32[1,16,256]{2,1,0:T(8,128)S(1)}, f32[1,16,256]{2,1,0:T(8,128)S(1)}, u32[]{:S(2)}, u32[]{:S(2)}) collective-permute-start(f32[1,16,256]{2,1,0:T(8,128)S(1)} %slice_bitcast_fusion.4), channel_id=1, source_target_pairs={{0,32},{32,64},{64,96},{96,128},{128,160},{160,192},{192,224},{224... | collective-permute-start | bytes 49160 | tf_op jit(solution)/shard_map/ppermute | solution.py:15
  64.5 1.5 pad_maximum_fusion
  66.0 2.0 collective-permute-start.5
  68.0 1.3 dynamic-slice
  70.0 0.7 gather_fusion
  70.6 0.7 gather_fusion.1
  71.3 0.7 gather_fusion.3
  72.0 0.7 gather_fusion.2
  72.6 4.3 %collective-permute-start.6 = (f32[1,16,256]{2,1,0:T(8,128)S(1)}, f32[1,16,256]{2,1,0:T(8,128)S(1)}, u32[]{:S(2)}, u32[]{:S(2)}) collective-permute-start(f32[1,16,256]{2,1,0:T(8,128)S(1)} %fusion.25), channel_id=1, source_target_pairs={{0,32},{32,64},{64,96},{96,128},{128,160},{160,192},{192,224},{224... | collective-permute-start | bytes 49160 | tf_op jit(solution)/shard_map/ppermute | solution.py:15
  77.0 0.8 collective-permute-done.6
  77.8 2.2 collective-permute-start.7
  80.0 0.6 pad_maximum_fusion.1
  80.8 30.4 %psum.7 = f32[1,16,256]{2,1,0:T(8,128)} all-reduce(f32[1,16,256]{2,1,0:T(8,128)S(1)} %fusion.23), channel_id=1, replica_groups=mesh['ctx'=16,'tis'=8,'rep'=4] {'tis'}, use_global_device_ids=true, to_apply=%region_10.12 | all-reduce | flops 4096 | bytes 32768 | tf_op jit(solution)/shard_map/psum | solution.py:110
  111.2 161.4 %all-reduce.4.cloned.1.call-done = f32[256,4,512]{2,0,1:T(8,128)} async-done(((f32[256,4,512]{2,0,1:T(8,128)}), f32[256,4,512]{2,0,1:T(8,128)}) %all-reduce.4.cloned.1.call-update) | async-done | bytes 2097168
  272.6 1.5 dynamic-slice_bitcast_fusion
  (65 shorter events, 3.7 us)
Async XLA Ops:
  7.2 20.0 %copy-start = (bf16[128,256]{1,0:T(8,128)(2,1)S(1)}, bf16[128,256]{1,0:T(8,128)(2,1)}, u32[]{:S(2)}) copy-start(bf16[128,256]{1,0:T(8,128)(2,1)} %param.17) | copy-start | bytes 196612
  7.2 265.4 %all-reduce.4.cloned.1.call-start = ((), (), s32[]{:S(2)}) async-start(), calls=%async_computation | async-start | bytes 4194304
  7.2 6.0 %collective-permute-start = (bf16[1,16,256]{2,1,0:T(8,128)(2,1)}, bf16[1,16,256]{2,1,0:T(8,128)(2,1)S(1)}, u32[]{:S(2)}, u32[]{:S(2)}) collective-permute-start(bf16[1,16,256]{2,1,0:T(8,128)(2,1)} %param.12), channel_id=1, source_target_pairs={{32,0},{64,32},{96,64},{128,96},{160,128},{192,160},{224,192},{256... | collective-permute-start | bytes 24584 | tf_op jit(solution)/shard_map/ppermute | solution.py:15
  13.2 3.7 %collective-permute-start.1 = (bf16[1,16,256]{2,1,0:T(8,128)(2,1)S(1)}, bf16[1,16,256]{2,1,0:T(8,128)(2,1)S(1)}, u32[]{:S(2)}, u32[]{:S(2)}) collective-permute-start(bf16[1,16,256]{2,1,0:T(8,128)(2,1)S(1)} %collective-permute-done), channel_id=1, source_target_pairs={{32,0},{64,32},{96,64},{128,96},{160,128},{192,160},{224,192},{256... | collective-permute-start | bytes 24584 | tf_op jit(solution)/shard_map/ppermute | solution.py:15
  16.9 5.2 %collective-permute-start.2 = (bf16[1,16,256]{2,1,0:T(8,128)(2,1)S(1)}, bf16[1,16,256]{2,1,0:T(8,128)(2,1)S(1)}, u32[]{:S(2)}, u32[]{:S(2)}) collective-permute-start(bf16[1,16,256]{2,1,0:T(8,128)(2,1)S(1)} %collective-permute-done.1), channel_id=1, source_target_pairs={{32,0},{64,32},{96,64},{128,96},{160,128},{192,160},{224,192},{256... | collective-permute-start | bytes 24584 | tf_op jit(solution)/shard_map/ppermute | solution.py:15
  22.2 5.0 %collective-permute-start.3 = (bf16[1,16,256]{2,1,0:T(8,128)(2,1)S(1)}, bf16[1,16,256]{2,1,0:T(8,128)(2,1)S(1)}, u32[]{:S(2)}, u32[]{:S(2)}) collective-permute-start(bf16[1,16,256]{2,1,0:T(8,128)(2,1)S(1)} %collective-permute-done.2), channel_id=1, source_target_pairs={{32,0},{64,32},{96,64},{128,96},{160,128},{192,160},{224,192},{256... | collective-permute-start | bytes 24584 | tf_op jit(solution)/shard_map/ppermute | solution.py:15
  27.1 1.7 copy-start.6
  34.3 2.3 copy-start.8
  37.1 1.7 copy-start.10
  37.2 1.7 copy-start.11
  55.5 1.3 copy-start.1
  55.5 1.6 copy-start.7
  58.3 1.3 copy-start.5
  58.9 5.6 %copy-start.2 = (f32[256,1,512]{2,0,1:T(8,128)S(1)}, f32[256,1,512]{2,0,1:T(8,128)}, u32[]{:S(2)}) copy-start(f32[256,1,512]{2,0,1:T(8,128)} %convolution_bitcast_fusion.3) | copy-start | bytes 1572868
  58.9 5.6 %copy-start.3 = (f32[256,1,512]{2,0,1:T(8,128)S(1)}, f32[256,1,512]{2,0,1:T(8,128)}, u32[]{:S(2)}) copy-start(f32[256,1,512]{2,0,1:T(8,128)} %convolution_bitcast_fusion) | copy-start | bytes 1572868
  58.9 5.6 %copy-start.4 = (f32[256,1,512]{2,0,1:T(8,128)S(1)}, f32[256,1,512]{2,0,1:T(8,128)}, u32[]{:S(2)}) copy-start(f32[256,1,512]{2,0,1:T(8,128)} %convolution_bitcast_fusion.1) | copy-start | bytes 1572868
  60.1 5.8 %collective-permute-start.4 = (f32[1,16,256]{2,1,0:T(8,128)S(1)}, f32[1,16,256]{2,1,0:T(8,128)S(1)}, u32[]{:S(2)}, u32[]{:S(2)}) collective-permute-start(f32[1,16,256]{2,1,0:T(8,128)S(1)} %slice_bitcast_fusion.4), channel_id=1, source_target_pairs={{0,32},{32,64},{64,96},{96,128},{128,160},{160,192},{192,224},{224... | collective-permute-start | bytes 49160 | tf_op jit(solution)/shard_map/ppermute | solution.py:15
  66.0 11.0 %copy-start.9 = (s32[1,16,4]{1,2,0:T(4,128)S(1)}, s32[1,16,4]{1,2,0:T(4,128)}, u32[]{:S(2)}) copy-start(s32[1,16,4]{1,2,0:T(4,128)} %param.16) | copy-start | bytes 772
  66.0 6.6 %collective-permute-start.5 = (f32[1,16,256]{2,1,0:T(8,128)S(1)}, f32[1,16,256]{2,1,0:T(8,128)S(1)}, u32[]{:S(2)}, u32[]{:S(2)}) collective-permute-start(f32[1,16,256]{2,1,0:T(8,128)S(1)} %fusion.26), channel_id=1, source_target_pairs={{0,32},{32,64},{64,96},{96,128},{128,160},{160,192},{192,224},{224... | collective-permute-start | bytes 49160 | tf_op jit(solution)/shard_map/ppermute | solution.py:15
  72.6 5.1 %collective-permute-start.6 = (f32[1,16,256]{2,1,0:T(8,128)S(1)}, f32[1,16,256]{2,1,0:T(8,128)S(1)}, u32[]{:S(2)}, u32[]{:S(2)}) collective-permute-start(f32[1,16,256]{2,1,0:T(8,128)S(1)} %fusion.25), channel_id=1, source_target_pairs={{0,32},{32,64},{64,96},{96,128},{128,160},{160,192},{192,224},{224... | collective-permute-start | bytes 49160 | tf_op jit(solution)/shard_map/ppermute | solution.py:15
  77.8 3.1 %collective-permute-start.7 = (f32[1,16,256]{2,1,0:T(8,128)S(1)}, f32[1,16,256]{2,1,0:T(8,128)S(1)}, u32[]{:S(2)}, u32[]{:S(2)}) collective-permute-start(f32[1,16,256]{2,1,0:T(8,128)S(1)} %fusion.24), channel_id=1, source_target_pairs={{0,32},{32,64},{64,96},{96,128},{128,160},{160,192},{192,224},{224... | collective-permute-start | bytes 49160 | tf_op jit(solution)/shard_map/ppermute | solution.py:15
Sparse Core Ops, SparseCore 0:
  66.1 206.4 all-reduce.3
where the time goes:
time: 282 us; the launch traced here: 281 us
  waiting for transfers between devices  172 us (61%)
  blocking collectives  30.4 us (11%)
  matrix products  20.5 us (7%)
  starting transfers between devices  18 us (6%)
  other arithmetic  15.4 us (5%)
  between operations  15.1 us (5%)
  local copies, waits for them, and re-layouts  9.11 us (3%)
    unnamed x2, waiting for transfers between devices  161 us
    psum x1, blocking collectives, on_device(): grad_acceptor = lax.psum(carried, 'tis')  30.4 us
    ppermute x8, starting transfers between devices, passed_along(): lax.ppermute(value, axis, [(source, source + steps) for source in range(f...  18 us
    ppermute x8, waiting for transfers between devices, passed_along(): lax.ppermute(value, axis, [(source, source + steps) for source in range(f...  11 us
    convert_element_type x4, other arithmetic, on_device(): grad_hid = (grad_act * silu_grad(hid)).astype(jnp.bfloat16)  9.15 us
    dot_general x4, matrix products, on_device(): hid = jnp.dot(flat, w_in, preferred_element_type=jnp.float32)  7.74 us
  transfers between devices with their start and end apart: 9, of which 6 were waited for; matrix products, arithmetic and copies ran while one was open for 4% of the time, Pallas kernels for 0%

commit v1 on v0

--- a/solution.py
+++ b/solution.py
@@ -107,7 +107,11 @@
     carried = contrib[:, reach - 1]
     for offset in range(reach - 2, -1, -1):
         carried = passed_along(carried, "ctx", 1) + contrib[:, offset]
-    grad_acceptor = lax.psum(carried, "tis")
+    grad_acceptor = carried
+    for hop in (1, 2, 4):
+        grad_acceptor = grad_acceptor + lax.ppermute(
+            grad_acceptor, "tis", [(dev, dev ^ hop) for dev in range(8)]
+        )
     donor_loss = jnp.stack(losses, axis=-1)
     return (donor_loss, grad_hidden, grad_acceptor)
 

time: 282 us -> 292 us (1.035)
  blocking collectives: 30.4 us -> 0 us
  waiting for transfers between devices: 172 us -> 199 us
  starting transfers between devices: 18 us -> 32.1 us
    psum x1 -> x0, blocking collectives: 30.4 us -> none  [on_device(): grad_acceptor = lax.psum(carried, 'tis')]
    unnamed x2, waiting for transfers between devices: 161 us -> 177 us
    ppermute x0 -> x3, starting transfers between devices: none -> 12 us  [on_device(): lax.ppermute(grad_acceptor, 'tis', [(dev, dev ^ hop) for dev in range(8)])]
    ppermute x0 -> x3, waiting for transfers between devices: none -> 10.8 us  [on_device(): lax.ppermute(grad_acceptor, 'tis', [(dev, dev ^ hop) for dev in range(8)])]
  transfers between devices with their start and end apart: 9 -> 12, of which waited for: 6 -> 9; matrix products, arithmetic and copies ran while one was open for 4% -> 4% of each run, Pallas kernels for 0% -> 0%
where the time goes in v1:
time: 292 us; the launch traced here: 291 us
  waiting for transfers between devices  199 us (68%)
  starting transfers between devices  32.1 us (11%)
  matrix products  18.9 us (6%)
  other arithmetic  16.1 us (6%)
  between operations  15.1 us (5%)
  local copies, waits for them, and re-layouts  9.26 us (3%)
    unnamed x2, waiting for transfers between devices  177 us
    ppermute x8, starting transfers between devices, passed_along(): lax.ppermute(value, axis, [(source, source + steps) for source in range(f...  20.1 us
    ppermute x3, starting transfers between devices, on_device(): lax.ppermute(grad_acceptor, 'tis', [(dev, dev ^ hop) for dev in range(8)])  12 us
    ppermute x8, waiting for transfers between devices, passed_along(): lax.ppermute(value, axis, [(source, source + steps) for source in range(f...  11.4 us
    ppermute x3, waiting for transfers between devices, on_device(): lax.ppermute(grad_acceptor, 'tis', [(dev, dev ^ hop) for dev in range(8)])  10.8 us
    convert_element_type x4, other arithmetic, on_device(): grad_hid = (grad_act * silu_grad(hid)).astype(jnp.bfloat16)  9.24 us
    dot_general x4, matrix products, on_device(): hid = jnp.dot(flat, w_in, preferred_element_type=jnp.float32)  9.22 us
  transfers between devices with their start and end apart: 12, of which 9 were waited for; matrix products, arithmetic and copies ran while one was open for 4% of the time, Pallas kernels for 0%

profile of v1, /device:TPU:8, one launch (start us, length us, event | category | flops | bytes accessed | tf_op | source)
XLA Modules:
  0.0 291.0 jit_solution(11426984809509607333)
XLA Ops:
  7.2 1.3 collective-permute-start
  8.5 0.7 constant_dynamic-update-slice_fusion.4
  9.2 0.7 bitcast_convert_fusion.1
  9.9 0.8 slice_bitcast_fusion.8
  10.8 0.9 slice_reduce_fusion.3
  11.6 0.8 bitcast_add_fusion.4
  12.4 0.7 fusion.28
  13.2 1.3 collective-permute-start.1
  14.5 2.4 collective-permute-done.1
  16.9 1.3 collective-permute-start.2
  18.2 3.9 %collective-permute-done.2 = bf16[1,16,256]{2,1,0:T(8,128)(2,1)S(1)} collective-permute-done((bf16[1,16,256]{2,1,0:T(8,128)(2,1)S(1)}, bf16[1,16,256]{2,1,0:T(8,128)(2,1)S(1)}, u32[]{:S(2)}, u32[]{:S(2)}) %collective-permute-start.2) | collective-permute-done | bytes 8224 | tf_op jit(solution)/shard_map/ppermute | solution.py:15
  22.1 1.3 collective-permute-start.3
  23.4 3.7 %collective-permute-done.3 = bf16[1,16,256]{2,1,0:T(8,128)(2,1)S(1)} collective-permute-done((bf16[1,16,256]{2,1,0:T(8,128)(2,1)S(1)}, bf16[1,16,256]{2,1,0:T(8,128)(2,1)S(1)}, u32[]{:S(2)}, u32[]{:S(2)}) %collective-permute-start.3) | collective-permute-done | bytes 8224 | tf_op jit(solution)/shard_map/ppermute | solution.py:15
  27.1 1.6 multiply_convert_fusion.8
  28.8 2.3 multiply_convert_fusion.7
  31.0 2.4 multiply_convert_fusion.4
  33.4 2.3 multiply_convert_fusion.5
  35.7 2.3 multiply_convert_fusion.6
  38.5 0.6 fusion.42
  39.1 0.6 fusion.44
  40.9 2.7 multiply_convert_fusion
  43.6 1.3 convolution_bitcast_fusion
  45.1 2.7 multiply_convert_fusion.1
  47.8 1.4 convolution_bitcast_fusion.1
  49.3 2.8 multiply_convert_fusion.3
  52.7 1.2 copy-done.1
  53.9 1.0 multiply_convert_fusion.2
  56.5 0.8 copy-done.4
  57.8 4.4 %collective-permute-start.4 = (f32[1,16,256]{2,1,0:T(8,128)S(1)}, f32[1,16,256]{2,1,0:T(8,128)S(1)}, u32[]{:S(2)}, u32[]{:S(2)}) collective-permute-start(f32[1,16,256]{2,1,0:T(8,128)S(1)} %slice_bitcast_fusion.4), channel_id=1, source_target_pairs={{0,32},{32,64},{64,96},{96,128},{128,160},{160,192},{192,224},{224... | collective-permute-start | bytes 49160 | tf_op jit(solution)/shard_map/ppermute | solution.py:15
  63.1 2.2 collective-permute-start.5
  66.1 4.1 %collective-permute-start.6 = (f32[1,16,256]{2,1,0:T(8,128)S(1)}, f32[1,16,256]{2,1,0:T(8,128)S(1)}, u32[]{:S(2)}, u32[]{:S(2)}) collective-permute-start(f32[1,16,256]{2,1,0:T(8,128)S(1)} %fusion.25), channel_id=1, source_target_pairs={{0,32},{32,64},{64,96},{96,128},{128,160},{160,192},{192,224},{224... | collective-permute-start | bytes 49160 | tf_op jit(solution)/shard_map/ppermute | solution.py:15
  70.2 1.5 pad_maximum_fusion
  71.7 4.2 %collective-permute-start.7 = (f32[1,16,256]{2,1,0:T(8,128)S(1)}, f32[1,16,256]{2,1,0:T(8,128)S(1)}, u32[]{:S(2)}, u32[]{:S(2)}) collective-permute-start(f32[1,16,256]{2,1,0:T(8,128)S(1)} %fusion.24), channel_id=1, source_target_pairs={{0,32},{32,64},{64,96},{96,128},{128,160},{160,192},{192,224},{224... | collective-permute-start | bytes 49160 | tf_op jit(solution)/shard_map/ppermute | solution.py:15
  76.0 0.8 collective-permute-done.7
  76.8 7.3 %collective-permute-start.8 = (f32[1,16,256]{2,1,0:T(8,128)S(1)}, f32[1,16,256]{2,1,0:T(8,128)S(1)}, u32[]{:S(2)}, u32[]{:S(2)}) collective-permute-start(f32[1,16,256]{2,1,0:T(8,128)S(1)} %fusion.23), channel_id=1, source_target_pairs={{0,4},{4,0},{8,12},{12,8},{16,20},{20,16},{24,28},{28,24},{1,5},{5... | collective-permute-start | bytes 49160 | tf_op jit(solution)/shard_map/ppermute | solution.py:112
  84.1 1.3 dynamic-slice
  86.1 0.7 gather_fusion
  86.7 0.7 gather_fusion.1
  87.4 0.7 gather_fusion.3
  88.0 0.7 gather_fusion.2
  88.7 1.9 collective-permute-start.9
  90.7 4.6 %collective-permute-done.9 = f32[1,16,256]{2,1,0:T(8,128)S(1)} collective-permute-done((f32[1,16,256]{2,1,0:T(8,128)S(1)}, f32[1,16,256]{2,1,0:T(8,128)S(1)}, u32[]{:S(2)}, u32[]{:S(2)}) %collective-permute-start.9) | collective-permute-done | bytes 16416 | tf_op jit(solution)/shard_map/ppermute | solution.py:112
  95.3 2.7 collective-permute-start.10
  98.0 0.6 pad_maximum_fusion.1
  98.6 6.2 %collective-permute-done.10 = f32[1,16,256]{2,1,0:T(8,128)S(1)} collective-permute-done((f32[1,16,256]{2,1,0:T(8,128)S(1)}, f32[1,16,256]{2,1,0:T(8,128)S(1)}, u32[]{:S(2)}, u32[]{:S(2)}) %collective-permute-start.10) | collective-permute-done | bytes 16416 | tf_op jit(solution)/shard_map/ppermute | solution.py:112
  104.8 0.6 add.302
  105.4 177.3 %all-reduce.4.cloned.1.call-done = f32[256,4,512]{2,0,1:T(8,128)} async-done(((f32[256,4,512]{2,0,1:T(8,128)}), f32[256,4,512]{2,0,1:T(8,128)}) %all-reduce.4.cloned.1.call-update) | async-done | bytes 2097168
  282.6 1.5 dynamic-slice_bitcast_fusion
  (71 shorter events, 6.5 us)
Async XLA Ops:
  7.2 20.0 %copy-start = (bf16[128,256]{1,0:T(8,128)(2,1)S(1)}, bf16[128,256]{1,0:T(8,128)(2,1)}, u32[]{:S(2)}) copy-start(bf16[128,256]{1,0:T(8,128)(2,1)} %param.17) | copy-start | bytes 196612
  7.2 275.5 %all-reduce.4.cloned.1.call-start = ((), (), s32[]{:S(2)}) async-start(), calls=%async_computation | async-start | bytes 4194304
  7.2 6.0 %collective-permute-start = (bf16[1,16,256]{2,1,0:T(8,128)(2,1)}, bf16[1,16,256]{2,1,0:T(8,128)(2,1)S(1)}, u32[]{:S(2)}, u32[]{:S(2)}) collective-permute-start(bf16[1,16,256]{2,1,0:T(8,128)(2,1)} %param.12), channel_id=1, source_target_pairs={{32,0},{64,32},{96,64},{128,96},{160,128},{192,160},{224,192},{256... | collective-permute-start | bytes 24584 | tf_op jit(solution)/shard_map/ppermute | solution.py:15
  13.2 3.7 %collective-permute-start.1 = (bf16[1,16,256]{2,1,0:T(8,128)(2,1)S(1)}, bf16[1,16,256]{2,1,0:T(8,128)(2,1)S(1)}, u32[]{:S(2)}, u32[]{:S(2)}) collective-permute-start(bf16[1,16,256]{2,1,0:T(8,128)(2,1)S(1)} %collective-permute-done), channel_id=1, source_target_pairs={{32,0},{64,32},{96,64},{128,96},{160,128},{192,160},{224,192},{256... | collective-permute-start | bytes 24584 | tf_op jit(solution)/shard_map/ppermute | solution.py:15
  16.9 5.2 %collective-permute-start.2 = (bf16[1,16,256]{2,1,0:T(8,128)(2,1)S(1)}, bf16[1,16,256]{2,1,0:T(8,128)(2,1)S(1)}, u32[]{:S(2)}, u32[]{:S(2)}) collective-permute-start(bf16[1,16,256]{2,1,0:T(8,128)(2,1)S(1)} %collective-permute-done.1), channel_id=1, source_target_pairs={{32,0},{64,32},{96,64},{128,96},{160,128},{192,160},{224,192},{256... | collective-permute-start | bytes 24584 | tf_op jit(solution)/shard_map/ppermute | solution.py:15
  22.1 5.0 %collective-permute-start.3 = (bf16[1,16,256]{2,1,0:T(8,128)(2,1)S(1)}, bf16[1,16,256]{2,1,0:T(8,128)(2,1)S(1)}, u32[]{:S(2)}, u32[]{:S(2)}) collective-permute-start(bf16[1,16,256]{2,1,0:T(8,128)(2,1)S(1)} %collective-permute-done.2), channel_id=1, source_target_pairs={{32,0},{64,32},{96,64},{128,96},{160,128},{192,160},{224,192},{256... | collective-permute-start | bytes 24584 | tf_op jit(solution)/shard_map/ppermute | solution.py:15
  27.1 1.6 copy-start.5
  35.7 2.3 copy-start.7
  38.5 1.7 copy-start.9
  38.5 1.7 copy-start.10
  49.3 2.8 copy-start.6
  52.1 1.7 copy-start.1
  55.9 1.3 copy-start.4
  57.7 12.4 %copy-start.2 = (f32[256,1,512]{2,0,1:T(8,128)S(1)}, f32[256,1,512]{2,0,1:T(8,128)}, u32[]{:S(2)}) copy-start(f32[256,1,512]{2,0,1:T(8,128)} %convolution_bitcast_fusion) | copy-start | bytes 1572868
  57.8 12.4 %copy-start.3 = (f32[256,1,512]{2,0,1:T(8,128)S(1)}, f32[256,1,512]{2,0,1:T(8,128)}, u32[]{:S(2)}) copy-start(f32[256,1,512]{2,0,1:T(8,128)} %convolution_bitcast_fusion.1) | copy-start | bytes 1572868
  57.8 5.3 %collective-permute-start.4 = (f32[1,16,256]{2,1,0:T(8,128)S(1)}, f32[1,16,256]{2,1,0:T(8,128)S(1)}, u32[]{:S(2)}, u32[]{:S(2)}) collective-permute-start(f32[1,16,256]{2,1,0:T(8,128)S(1)} %slice_bitcast_fusion.4), channel_id=1, source_target_pairs={{0,32},{32,64},{64,96},{96,128},{128,160},{160,192},{192,224},{224... | collective-permute-start | bytes 49160 | tf_op jit(solution)/shard_map/ppermute | solution.py:15
  63.1 3.1 %collective-permute-start.5 = (f32[1,16,256]{2,1,0:T(8,128)S(1)}, f32[1,16,256]{2,1,0:T(8,128)S(1)}, u32[]{:S(2)}, u32[]{:S(2)}) collective-permute-start(f32[1,16,256]{2,1,0:T(8,128)S(1)} %fusion.26), channel_id=1, source_target_pairs={{0,32},{32,64},{64,96},{96,128},{128,160},{160,192},{192,224},{224... | collective-permute-start | bytes 49160 | tf_op jit(solution)/shard_map/ppermute | solution.py:15
  66.1 5.6 %collective-permute-start.6 = (f32[1,16,256]{2,1,0:T(8,128)S(1)}, f32[1,16,256]{2,1,0:T(8,128)S(1)}, u32[]{:S(2)}, u32[]{:S(2)}) collective-permute-start(f32[1,16,256]{2,1,0:T(8,128)S(1)} %fusion.25), channel_id=1, source_target_pairs={{0,32},{32,64},{64,96},{96,128},{128,160},{160,192},{192,224},{224... | collective-permute-start | bytes 49160 | tf_op jit(solution)/shard_map/ppermute | solution.py:15
  71.7 19.0 %copy-start.8 = (s32[1,16,4]{1,2,0:T(4,128)S(1)}, s32[1,16,4]{1,2,0:T(4,128)}, u32[]{:S(2)}) copy-start(s32[1,16,4]{1,2,0:T(4,128)} %param.16) | copy-start | bytes 772
  71.7 5.0 %collective-permute-start.7 = (f32[1,16,256]{2,1,0:T(8,128)S(1)}, f32[1,16,256]{2,1,0:T(8,128)S(1)}, u32[]{:S(2)}, u32[]{:S(2)}) collective-permute-start(f32[1,16,256]{2,1,0:T(8,128)S(1)} %fusion.24), channel_id=1, source_target_pairs={{0,32},{32,64},{64,96},{96,128},{128,160},{160,192},{192,224},{224... | collective-permute-start | bytes 49160 | tf_op jit(solution)/shard_map/ppermute | solution.py:15
  76.8 11.9 %collective-permute-start.8 = (f32[1,16,256]{2,1,0:T(8,128)S(1)}, f32[1,16,256]{2,1,0:T(8,128)S(1)}, u32[]{:S(2)}, u32[]{:S(2)}) collective-permute-start(f32[1,16,256]{2,1,0:T(8,128)S(1)} %fusion.23), channel_id=1, source_target_pairs={{0,4},{4,0},{8,12},{12,8},{16,20},{20,16},{24,28},{28,24},{1,5},{5... | collective-permute-start | bytes 49160 | tf_op jit(solution)/shard_map/ppermute | solution.py:112
  88.7 6.5 %collective-permute-start.9 = (f32[1,16,256]{2,1,0:T(8,128)S(1)}, f32[1,16,256]{2,1,0:T(8,128)S(1)}, u32[]{:S(2)}, u32[]{:S(2)}) collective-permute-start(f32[1,16,256]{2,1,0:T(8,128)S(1)} %add.300), channel_id=1, source_target_pairs={{0,8},{4,12},{8,0},{12,4},{16,24},{20,28},{24,16},{28,20},{1,9},{5... | collective-permute-start | bytes 49160 | tf_op jit(solution)/shard_map/ppermute | solution.py:112
  95.3 9.5 %collective-permute-start.10 = (f32[1,16,256]{2,1,0:T(8,128)S(1)}, f32[1,16,256]{2,1,0:T(8,128)S(1)}, u32[]{:S(2)}, u32[]{:S(2)}) collective-permute-start(f32[1,16,256]{2,1,0:T(8,128)S(1)} %add.301), channel_id=1, source_target_pairs={{0,16},{4,20},{8,24},{12,28},{16,0},{20,4},{24,8},{28,12},{1,17},{... | collective-permute-start | bytes 49160 | tf_op jit(solution)/shard_map/ppermute | solution.py:112
Sparse Core Ops, SparseCore 0:
  71.8 210.7 all-reduce.3
